TPU v7x, 32 devices: a whole 2x2x4 slice. The times are simulated.
32 devices in a mesh: seq: 4 (over z), exp: 2 (over core), hid: 4 (over y, x).
Axes of the slice: x: 2, y: 2, z: 4, core: 2. Of those that a mesh axis runs over, the one named last changes fastest.
Arguments:
- tokens: bfloat16 [512, 6144], P('seq'), may hold values from -6 to 6
- out_grad: bfloat16 [512, 6144], P('seq'), may hold values from -3 to 3
- expert_ids: int32 [512, 2], P('seq'), may hold values from 0 to 7, as said below
- gate_probs: float32 [512, 2], P('seq'), may hold values from 0.1 to 1
- w_gate: bfloat16 [2, 6144, 16384], P('exp', None, ('seq', 'hid')), may hold values from -0.078125 to 0.078125
- w_up: bfloat16 [2, 6144, 16384], P('exp', None, ('seq', 'hid')), may hold values from -0.078125 to 0.078125
- w_down: bfloat16 [2, 16384, 6144], P('exp', ('seq', 'hid')), may hold values from -0.046875 to 0.046875
Outputs:
- d_w_gate: bfloat16 [2, 6144, 16384], P('exp', None, ('seq', 'hid'))
- d_w_up: bfloat16 [2, 6144, 16384], P('exp', None, ('seq', 'hid'))
- d_w_down: bfloat16 [2, 16384, 6144], P('exp', ('seq', 'hid'))
- d_tokens: float32 [512, 6144], P('seq', 'hid')
- d_gates: float32 [512, 2], P('seq')
Inputs may be any that keep to these rules, and one draw needn't show every extreme that they name: `expert_ids`: in each block of 128 rows (the tokens of one index of seq) the two ids of a row differ and no expert is named more than 40 times; each expert below 2 is named 40 // 2 to 40 times in a block, exactly 40 times in the first block.
All inputs are finite; a program needn't handle non-finite values.
Results may differ from a plain program's by a relative error of at most 0.015.
Values may be sent and summed in bfloat16 or wider, within the bound.
No kernel may reach another device: no remote copies, remote signals or barrier semaphores. Data moves between devices by JAX's collectives and lax.ppermute only.
A program may use at most 192 MiB of HBM per device.

v0:
```python
import jax
import jax.numpy as jnp
from jax import lax
from jax.sharding import PartitionSpec as P


def on_device(tokens, out_grad, expert_ids, gate_probs, w_gate, w_up, w_down):
    expert = lax.axis_index("exp")
    tok_rows = tokens.shape[0]
    model_width = tokens.shape[1]
    capacity = 5 * tok_rows // 16
    seq_count = lax.axis_size("seq")
    hid_count = lax.axis_size("hid")
    piece_width = model_width // hid_count
    hidden_local = w_gate.shape[2]
    chosen = (expert_ids == expert).astype(jnp.int32)
    slot_index = (jnp.cumsum(chosen.reshape(-1)) - 1).reshape(tok_rows, 2)
    columns = jnp.arange(capacity, dtype=jnp.int32)
    pick_table = (
        (chosen[:, :, None] == 1) & (slot_index[:, :, None] == columns[None, None, :])
    ).astype(jnp.float32)
    select_rows = jnp.sum(pick_table, axis=1)
    select_half = select_rows.astype(jnp.bfloat16)
    contract_rows = (((0,), (0,)), ((), ()))
    token_slots = lax.dot_general(
        select_half, tokens, contract_rows, preferred_element_type=jnp.float32
    ).astype(jnp.bfloat16)
    grad_slots = lax.dot_general(
        select_half, out_grad, contract_rows, preferred_element_type=jnp.float32
    ).astype(jnp.bfloat16)
    weight_slots = jnp.sum(pick_table * gate_probs[:, :, None], axis=(0, 1))
    rows_e, grads_e, weight_e = (
        lax.all_gather(token_slots, "seq", axis=0, tiled=True),
        lax.all_gather(grad_slots, "seq", axis=0, tiled=True),
        lax.all_gather(weight_slots.astype(jnp.bfloat16), "seq", axis=0, tiled=True).astype(
            weight_slots.dtype
        ),
    )
    gate_mat = w_gate[0]
    up_mat = w_up[0]
    down_mat = w_down[0]
    gate_pre = jnp.dot(rows_e, gate_mat, preferred_element_type=jnp.float32)
    up_pre = jnp.dot(rows_e, up_mat, preferred_element_type=jnp.float32)
    sig_gate = jax.nn.sigmoid(gate_pre)
    activated = gate_pre * sig_gate
    hidden = (activated * up_pre).astype(jnp.bfloat16)
    back_hidden = lax.dot_general(
        grads_e, down_mat, (((1,), (1,)), ((), ())), preferred_element_type=jnp.float32
    )
    slot_part = jnp.sum(hidden.astype(jnp.float32) * back_hidden, axis=1)
    weighted = (weight_e[:, None] * hidden.astype(jnp.float32)).astype(jnp.bfloat16)
    grad_down = lax.dot_general(
        weighted, grads_e, contract_rows, preferred_element_type=jnp.float32
    ).astype(jnp.bfloat16)
    scaled_back = weight_e[:, None] * back_hidden
    d_gate = (scaled_back * up_pre * (sig_gate * (1.0 + gate_pre * (1.0 - sig_gate)))).astype(
        jnp.bfloat16
    )
    d_up = (scaled_back * activated).astype(jnp.bfloat16)
    grad_gate = lax.dot_general(
        rows_e, d_gate, contract_rows, preferred_element_type=jnp.float32
    ).astype(jnp.bfloat16)
    grad_up = lax.dot_general(
        rows_e, d_up, contract_rows, preferred_element_type=jnp.float32
    ).astype(jnp.bfloat16)
    gate_blocks = d_gate.reshape(seq_count, capacity, hidden_local)
    up_blocks = d_up.reshape(seq_count, capacity, hidden_local)
    partials = jnp.einsum(
        "sqf,hcf->shqc",
        gate_blocks,
        gate_mat.reshape(hid_count, piece_width, hidden_local),
        preferred_element_type=jnp.float32,
    )
    partials = partials + jnp.einsum(
        "sqf,hcf->shqc",
        up_blocks,
        up_mat.reshape(hid_count, piece_width, hidden_local),
        preferred_element_type=jnp.float32,
    )
    slot_terms = jnp.broadcast_to(
        slot_part.reshape(seq_count, 1, capacity), (seq_count, hid_count, capacity)
    )
    flat_parts = partials.reshape(seq_count * hid_count, capacity, piece_width)
    flat_slots = slot_terms.reshape(seq_count * hid_count, capacity)
    partials, slot_terms = (
        lax.psum_scatter(flat_parts, ("seq", "hid"), scatter_dimension=0, tiled=True),
        lax.psum_scatter(flat_slots, ("seq", "hid"), scatter_dimension=0, tiled=True),
    )
    own_rows = partials.reshape(capacity, piece_width)
    slot_grad = slot_terms.reshape(capacity)
    token_part = jnp.dot(
        select_rows, own_rows, precision=lax.Precision.HIGHEST, preferred_element_type=jnp.float32
    )
    gate_part = jnp.sum(pick_table * slot_grad[None, None, :], axis=2)
    token_sum, gate_sum = (
        lax.psum(token_part.astype(jnp.bfloat16), "exp").astype(jnp.float32),
        lax.psum(gate_part.astype(jnp.bfloat16), "exp").astype(jnp.float32),
    )
    return (grad_gate[None], grad_up[None], grad_down[None], token_sum, gate_sum)


def solution(mesh):
    return jax.shard_map(
        on_device,
        mesh=mesh,
        in_specs=(
            P("seq", None),
            P("seq", None),
            P("seq", None),
            P("seq", None),
            P("exp", None, ("seq", "hid")),
            P("exp", None, ("seq", "hid")),
            P("exp", ("seq", "hid"), None),
        ),
        out_specs=(
            P("exp", None, ("seq", "hid")),
            P("exp", None, ("seq", "hid")),
            P("exp", ("seq", "hid"), None),
            P("seq", "hid"),
            P("seq", None),
        ),
        check_vma=False,
    )
```

profile of v0, /device:TPU:0, one launch (start us, length us, event | category | flops | bytes accessed | tf_op | source)
XLA Modules:
  0.0 344.5 jit_solution(5438517381305366996)
XLA Ops:
  7.2 0.0 copy-start
  7.2 0.0 copy-start.11
  7.2 0.0 copy-start.10
  7.2 0.0 all-gather.3.cloned.1.call-start
  7.3 0.8 broadcast_compare_fusion
  8.0 0.1 copy.22
  8.2 0.1 reshape.70
  8.3 0.3 reduce-window.9
  8.6 0.1 reshape.71
  8.8 0.1 slice.7
  8.8 0.1 copy.23
  8.9 0.1 slice_reduce_fusion
  9.1 0.1 broadcast.33
  9.1 0.1 reshape.73
  9.3 1.1 convolution_convert_fusion.1
  10.4 0.0 all-gather.3.cloned.1.call-update
  10.4 0.0 all-gather.5.cloned.1.call-start
  10.5 2.5 convolution_convert_fusion
  13.0 0.0 all-gather.5.cloned.1.call-update
  13.0 0.0 reduce-scatter.2.cloned.1.call-start
  13.1 0.6 dynamic-slice.1
  13.7 0.6 dynamic-slice
  14.9 41.9 %all-gather.3.cloned.1.call-done = bf16[160,6144]{1,0:T(8,128)(2,1)} async-done(((bf16[40,6144]{1,0:T(8,128)(2,1)}), bf16[160,6144]{1,0:T(8,128)(2,1)}) %all-gather.3.cloned.1.call-update) | async-done | bytes 1966096 | tf_op jit(solution)/shard_map/all_gather | solution.py:33
  56.8 7.5 %fusion = f32[160,1024]{1,0:T(8,128)S(1)} fusion(bf16[160,6144]{1,0:T(8,128)(2,1)} %all-gather.3.cloned.1.call-done, bf16[1,6144,1024]{2,1,0:T(8,128)(2,1)} %param.11), kind=kOutput, calls=%fused_computation | convolution fusion | flops 2013265920 | bytes 15204352 | tf_op jit(solution)/shard_map/dot_general | solution.py:42
  64.4 7.1 %fusion.2 = f32[160,1024]{1,0:T(8,128)S(1)} fusion(bf16[160,6144]{1,0:T(8,128)(2,1)S(1)} %copy-done.2, bf16[1,6144,1024]{2,1,0:T(8,128)(2,1)} %param.12), kind=kOutput, calls=%fused_computation.2 | convolution fusion | flops 2013265920 | bytes 15204352 | tf_op jit(solution)/shard_map/dot_general | solution.py:43
  71.5 29.9 %all-gather.5.cloned.1.call-done = bf16[160,6144]{1,0:T(8,128)(2,1)} async-done(((bf16[40,6144]{1,0:T(8,128)(2,1)}), bf16[160,6144]{1,0:T(8,128)(2,1)}) %all-gather.5.cloned.1.call-update) | async-done | bytes 1966096 | tf_op jit(solution)/shard_map/all_gather | solution.py:34
  101.4 10.4 %fusion.7 = (f32[160]{0:T(256)S(1)}, bf16[160,1024]{1,0:T(8,128)(2,1)}, f32[160,1024]{1,0:T(8,128)}) fusion(f32[160,1024]{1,0:T(8,128)S(1)} %fusion.2, f32[160,1024]{1,0:T(8,128)S(1)} %fusion, bf16[160,6144]{1,0:T(8,128)(2,1)} %all-gather.5.cloned.1.call-done, bf16[1,1024,6144]{2,1,0:T(8,128)(2,1)} %param.13), kind=kOutput, calls=%fused_computation.16 | convolution fusion | flops 2014740352 | bytes 16843392 | tf_op jit(solution)/shard_map/dot_general | solution.py:47
  111.8 0.1 broadcast_in_dim.24
  111.9 40.0 %all-reduce.1 = f32[16,40]{1,0:T(8,128)S(1)} all-reduce(f32[16,40]{1,0:T(8,128)S(1)} %bitcast.64), channel_id=3, replica_groups=mesh['seq'=4,'exp'=2,'hid'=4] {'seq','hid'}, use_global_device_ids=true, to_apply=%region_7.8.clone | all-reduce | flops 640 | bytes 5120
  151.9 0.7 dynamic-slice_bitcast_fusion
  152.6 0.1 select_reduce_fusion
  152.7 0.2 dynamic-update-slice
  153.0 8.5 %all-reduce = bf16[160]{0:T(256)(128)(2,1)S(1)} all-reduce(bf16[160]{0:T(256)(128)(2,1)S(1)} %dynamic-update-slice), channel_id=1, replica_groups=mesh['seq'=4,'exp'=2,'hid'=4] {'seq'}, use_global_device_ids=true, to_apply=%add | all-reduce | flops 160 | bytes 640
  161.5 1.4 multiply_convert_fusion.1
  163.0 9.0 %fusion.15 = f32[4,40,4,1536]{3,1,2,0:T(8,128)S(1)} fusion(bf16[4,40,1024,1]{2,1,3,0:T(8,128)(2,1)S(1)} %bitcast.62, bf16[4,1536,1024,1]{2,1,0,3:T(8,128)(2,1)} %bitcast.59), kind=kOutput, calls=%fused_computation.36 | convolution fusion | flops 2013265920 | bytes 16842752 | tf_op jit(solution)/shard_map/sqf,hcf->shqc/dot_general | solution.py:68
  172.0 10.8 %convolution_add_fusion = f32[4,40,4,1536]{3,1,2,0:T(8,128)} fusion(f32[4,40,4,1536]{3,1,2,0:T(8,128)S(1)} %fusion.15, bf16[4,40,1024,1]{2,1,3,0:T(8,128)(2,1)S(1)} %bitcast.63, bf16[4,1536,1024,1]{2,1,0,3:T(8,128)(2,1)} %bitcast.60), kind=kOutput, calls=%fused_computation.11 | convolution fusion | flops 2014248960 | bytes 20774912 | tf_op jit(solution)/shard_map/sqf,hcf->shqc/dot_general | solution.py:74
  182.8 0.0 reduce-scatter.2.cloned.1.call-update
  182.8 0.0 all-reduce.4.cloned.1.call-start
  182.9 2.7 psum.15
  185.6 0.6 convert_element_type.76
  186.2 6.6 %convert_bitcast_fusion.1 = bf16[1,6144,1024]{2,1,0:T(8,128)(2,1)} fusion(bf16[160,6144]{1,0:T(8,128)(2,1)S(1)} %copy-done.2, bf16[160,1024]{1,0:T(8,128)(2,1)S(1)} %copy-done.8), kind=kOutput, calls=%fused_computation.7 | convolution fusion | flops 2019557376 | bytes 14876672 | tf_op jit(solution)/shard_map/dot_general | solution.py:63
  192.8 6.6 %convert_bitcast_fusion.2 = bf16[1,6144,1024]{2,1,0:T(8,128)(2,1)} fusion(bf16[160,6144]{1,0:T(8,128)(2,1)S(1)} %copy-done.2, bf16[160,1024]{1,0:T(8,128)(2,1)S(1)} %copy-done.6), kind=kOutput, calls=%fused_computation.8 | convolution fusion | flops 2019557376 | bytes 14876672 | tf_op jit(solution)/shard_map/dot_general | solution.py:60
  199.4 116.0 %reduce-scatter.2.cloned.1.call-done = f32[1,40,1536]{2,1,0:T(8,128)} async-done(((f32[16,40,1536]{2,1,0:T(8,128)}), f32[1,40,1536]{2,1,0:T(8,128)}) %reduce-scatter.2.cloned.1.call-update) | async-done | bytes 245776 | tf_op jit(solution)/shard_map/reduce_scatter | solution.py:86
  315.5 2.5 convolution_convert_fusion.2
  318.0 0.0 all-reduce.4.cloned.1.call-update
  318.0 10.1 %convert_bitcast_fusion = bf16[1,1024,6144]{2,1,0:T(8,128)(2,1)} fusion(bf16[160,6144]{1,0:T(8,128)(2,1)} %all-gather.5.cloned.1.call-done, bf16[160,1024]{1,0:T(8,128)(2,1)} %get-tuple-element.8, f32[160]{0:T(256)S(1)} %convert_element_type.63), kind=kOutput, calls=%fused_computation.6 | convolution fusion | flops 2020048896 | bytes 14877312 | tf_op jit(solution)/shard_map/dot_general | solution.py:52
  328.1 7.9 %all-reduce.4.cloned.1.call-done = bf16[128,1536]{1,0:T(8,128)(2,1)} async-done(((bf16[128,1536]{1,0:T(8,128)(2,1)}), bf16[128,1536]{1,0:T(8,128)(2,1)}) %all-reduce.4.cloned.1.call-update) | async-done | bytes 393232 | tf_op jit(solution)/shard_map/psum | solution.py:96
  336.1 2.0 convert_element_type.74
  (27 shorter events, 0.1 us)
Async XLA Ops:
  7.2 2.1 copy-start
  7.2 5.9 %copy-start.11 = (u32[32]{0:T(128)S(1)}, u32[32]{0:T(128)}, u32[]{:S(2)}) copy-start(u32[32]{0:T(128)} %constant.32) | copy-start | bytes 388
  7.2 6.5 %copy-start.10 = (u32[32]{0:T(128)S(1)}, u32[32]{0:T(128)}, u32[]{:S(2)}) copy-start(u32[32]{0:T(128)} %constant.26) | copy-start | bytes 388
  7.2 49.6 %all-gather.3.cloned.1.call-start = ((), (), s32[]{:S(2)}) async-start(), calls=%async_computation.1 | async-start | bytes 2457600 | tf_op jit(solution)/shard_map/all_gather | solution.py:33
  9.3 5.7 %copy-start.3 = (f32[128,40]{0,1:T(8,128)}, f32[128,40]{0,1:T(8,128)S(1)}, u32[]{:S(2)}) copy-start(f32[128,40]{0,1:T(8,128)S(1)} %convert_reduce_fusion) | copy-start | bytes 61444
  10.4 91.0 %all-gather.5.cloned.1.call-start = ((), (), s32[]{:S(2)}) async-start(), calls=%async_computation.2 | async-start | bytes 2457600 | tf_op jit(solution)/shard_map/all_gather | solution.py:34
  13.0 302.4 %reduce-scatter.2.cloned.1.call-start = ((), (), s32[]{:S(2)}) async-start(), calls=%async_computation.3 | async-start | bytes 4177920 | tf_op jit(solution)/shard_map/reduce_scatter | solution.py:86
  56.8 7.5 %copy-start.2 = (bf16[160,6144]{1,0:T(8,128)(2,1)S(1)}, bf16[160,6144]{1,0:T(8,128)(2,1)}, u32[]{:S(2)}) copy-start(bf16[160,6144]{1,0:T(8,128)(2,1)} %all-gather.3.cloned.1.call-done) | copy-start | bytes 5898244
  71.5 81.1 %copy-start.9 = (f32[128,2]{0,1:T(2,128)S(1)}, f32[128,2]{0,1:T(2,128)}, u32[]{:S(2)}) copy-start(f32[128,2]{0,1:T(2,128)} %param.10) | copy-start | bytes 3076
  163.0 9.0 %copy-start.5 = (bf16[160,1024]{1,0:T(8,128)(2,1)}, bf16[160,1024]{1,0:T(8,128)(2,1)S(1)}, u32[]{:S(2)}) copy-start(bf16[160,1024]{1,0:T(8,128)(2,1)S(1)} %get-tuple-element.12) | copy-start | bytes 983044
  163.0 9.0 %copy-start.7 = (bf16[160,1024]{1,0:T(8,128)(2,1)}, bf16[160,1024]{1,0:T(8,128)(2,1)S(1)}, u32[]{:S(2)}) copy-start(bf16[160,1024]{1,0:T(8,128)(2,1)S(1)} %get-tuple-element.11) | copy-start | bytes 983044
  182.8 3.3 copy-start.8
  182.8 153.2 %all-reduce.4.cloned.1.call-start = ((), (), s32[]{:S(2)}) async-start(), calls=%async_computation.4 | async-start | bytes 786432 | tf_op jit(solution)/shard_map/psum | solution.py:96
  186.2 6.6 %copy-start.6 = (bf16[160,1024]{1,0:T(8,128)(2,1)S(1)}, bf16[160,1024]{1,0:T(8,128)(2,1)}, u32[]{:S(2)}) copy-start(bf16[160,1024]{1,0:T(8,128)(2,1)} %copy-done.5) | copy-start | bytes 983044
  192.8 122.7 %copy-start.4 = (f32[128,40]{0,1:T(8,128)S(1)}, f32[128,40]{0,1:T(8,128)}, u32[]{:S(2)}) copy-start(f32[128,40]{0,1:T(8,128)} %copy-done.3) | copy-start | bytes 61444
  318.0 20.0 %copy-start.1 = (bf16[128,6144]{1,0:T(8,128)(2,1)S(1)}, bf16[128,6144]{1,0:T(8,128)(2,1)}, u32[]{:S(2)}) copy-start(bf16[128,6144]{1,0:T(8,128)(2,1)} %param.7) | copy-start | bytes 4718596
Sparse Core Ops, SparseCore 0:
  10.5 46.2 all-gather.2
  59.0 42.3 all-gather.4
  183.0 132.4 reduce-scatter.1
  318.2 17.7 all-reduce.3
where the time goes:
time: 345 us
  waiting for transfers between devices  196 us (57%)
  matrix products  74.3 us (22%)
  blocking collectives  51.3 us (15%)
  between operations  14.6 us (4%)
  other arithmetic  5.25 us (2%)
    reduce_scatter x1, waiting for transfers between devices, on_device(): lax.psum_scatter(flat_parts, ('seq', 'hid'), scatter_dimension=0, tiled=T...  116 us
    unnamed x2, blocking collectives  48.6 us
    all_gather x1, waiting for transfers between devices, on_device(): lax.all_gather(token_slots, 'seq', axis=0, tiled=True)  41.9 us
    all_gather x1, waiting for transfers between devices, on_device(): lax.all_gather(grad_slots, 'seq', axis=0, tiled=True)  29.9 us
    dot_general x1, matrix products, on_device(): jnp.einsum('sqf,hcf->shqc', up_blocks, up_mat.reshape(hid_count, piece_wi...  10.8 us
    dot_general x1, matrix products, on_device(): lax.dot_general(grads_e, down_mat, (((1,), (1,)), ((), ())), preferred_el...  10.4 us
    dot_general x1, matrix products, on_device(): lax.dot_general(weighted, grads_e, contract_rows, preferred_element_type=...  10.1 us
    dot_general x1, matrix products, on_device(): jnp.einsum('sqf,hcf->shqc', gate_blocks, gate_mat.reshape(hid_count, piec...  9.01 us
  transfers between devices with their start and end apart: 4, of which 4 were waited for; matrix products, arithmetic and copies ran while one was open for 12% of the time, Pallas kernels for 0%

commit v1 on v0

--- a/solution.py
+++ b/solution.py
@@ -2,6 +2,27 @@
 import jax.numpy as jnp
 from jax import lax
 from jax.sharding import PartitionSpec as P
+
+
+def ring_gather(array, axis, dim):
+    size, mine, extent = (lax.axis_size(axis), lax.axis_index(axis), array.shape[dim])
+    right = [(i, (i + 1) % size) for i in range(size)]
+    behind = [(i, (i - 1) % size) for i in range(size)]
+    result = jnp.zeros((*array.shape[:dim], size * extent, *array.shape[dim + 1 :]), array.dtype)
+    result = lax.dynamic_update_slice_in_dim(result, array, mine * extent, axis=dim)
+    from_left = from_right = array
+    middle = size // 2
+    for step in range(1, middle + 1):
+        from_left = lax.ppermute(from_left, axis, right)
+        result = lax.dynamic_update_slice_in_dim(
+            result, from_left, (mine - step) % size * extent, axis=dim
+        )
+        if step < size - middle:
+            from_right = lax.ppermute(from_right, axis, behind)
+            result = lax.dynamic_update_slice_in_dim(
+                result, from_right, (mine + step) % size * extent, axis=dim
+            )
+    return result
 
 
 def on_device(tokens, out_grad, expert_ids, gate_probs, w_gate, w_up, w_down):
@@ -30,7 +51,7 @@
     ).astype(jnp.bfloat16)
     weight_slots = jnp.sum(pick_table * gate_probs[:, :, None], axis=(0, 1))
     rows_e, grads_e, weight_e = (
-        lax.all_gather(token_slots, "seq", axis=0, tiled=True),
+        ring_gather(token_slots, "seq", 0),
         lax.all_gather(grad_slots, "seq", axis=0, tiled=True),
         lax.all_gather(weight_slots.astype(jnp.bfloat16), "seq", axis=0, tiled=True).astype(
             weight_slots.dtype

time: 345 us -> 326 us (0.945)
  waiting for transfers between devices: 196 us -> 176 us
  matrix products: 74.3 us -> 67.4 us
  starting transfers between devices: 0.16 us -> 5.65 us
    ppermute x0 -> x3, waiting for transfers between devices: none -> 48.9 us  [the longest x1 38.1 us: ring_gather(): from_right = lax.ppermute(from_right, axis, behind)]
    all_gather x1 -> x0, waiting for transfers between devices: 41.9 us -> none  [on_device(): lax.all_gather(token_slots, 'seq', axis=0, tiled=True)]
    all_gather x1, waiting for transfers between devices: 29.9 us -> 2.64 us  [on_device(): lax.all_gather(grad_slots, 'seq', axis=0, tiled=True)]
    ppermute x0 -> x3, starting transfers between devices: none -> 5.53 us  [the longest x2 3.5 us: ring_gather(): from_left = lax.ppermute(from_left, axis, right)]
    dot_general x1, matrix products: 7.11 us -> 2.19 us  [on_device(): up_pre = jnp.dot(rows_e, up_mat, preferred_element_type=jnp.float32)]
  transfers between devices with their start and end apart: 4 -> 6, of which waited for: 4 -> 6; matrix products, arithmetic and copies ran while one was open for 12% -> 11% of each run, Pallas kernels for 0% -> 0%
where the time goes in v1:
time: 326 us; the launch traced here: 325 us
  waiting for transfers between devices  176 us (54%)
  matrix products  67.4 us (21%)
  blocking collectives  52.9 us (16%)
  between operations  14.7 us (5%)
  starting transfers between devices  5.65 us (2%)
  other arithmetic  5.26 us (2%)
  local copies, waits for them, and re-layouts  3.47 us (1%)
    reduce_scatter x1, waiting for transfers between devices, on_device(): lax.psum_scatter(flat_parts, ('seq', 'hid'), scatter_dimension=0, tiled=T...  116 us
    unnamed x2, blocking collectives  50.2 us
    ppermute x1, waiting for transfers between devices, ring_gather(): from_right = lax.ppermute(from_right, axis, behind)  38.1 us
    dot_general x1, matrix products, on_device(): jnp.einsum('sqf,hcf->shqc', up_blocks, up_mat.reshape(hid_count, piece_wi...  10.8 us
    ppermute x2, waiting for transfers between devices, ring_gather(): from_left = lax.ppermute(from_left, axis, right)  10.8 us
    dot_general x1, matrix products, on_device(): lax.dot_general(grads_e, down_mat, (((1,), (1,)), ((), ())), preferred_el...  10.4 us
    dot_general x1, matrix products, on_device(): lax.dot_general(weighted, grads_e, contract_rows, preferred_element_type=...  10.1 us
    dot_general x1, matrix products, on_device(): jnp.einsum('sqf,hcf->shqc', gate_blocks, gate_mat.reshape(hid_count, piec...  9.01 us
  transfers between devices with their start and end apart: 6, of which 6 were waited for; matrix products, arithmetic and copies ran while one was open for 11% of the time, Pallas kernels for 0%

profile of v1, /device:TPU:0, one launch (start us, length us, event | category | flops | bytes accessed | tf_op | source)
XLA Modules:
  0.0 325.2 jit_solution(1377726241596858932)
XLA Ops:
  7.2 0.0 all-gather.2.cloned.1.call-start
  7.2 0.8 broadcast_compare_fusion
  8.0 0.1 copy.22
  8.1 0.1 reshape.70
  8.3 0.3 reduce-window.9
  8.6 0.1 reshape.71
  8.7 0.1 slice.7
  8.8 0.1 copy.23
  8.9 0.1 slice_reduce_fusion
  9.0 0.1 broadcast.36
  9.1 0.1 reshape.73
  9.3 0.2 broadcast_in_dim.24
  9.5 1.1 constant_dynamic-update-slice_fusion.3
  10.6 3.0 collective-permute-start
  13.6 2.0 collective-permute-start.1
  15.7 1.1 convolution_convert_fusion
  16.8 0.0 all-gather.2.cloned.1.call-update
  16.8 0.0 reduce-scatter.2.cloned.1.call-start
  16.9 0.6 dynamic-slice.1
  17.5 0.6 dynamic-slice
  18.8 9.2 %collective-permute-done = bf16[40,6144]{1,0:T(8,128)(2,1)S(1)} collective-permute-done((bf16[40,6144]{1,0:T(8,128)(2,1)}, bf16[40,6144]{1,0:T(8,128)(2,1)S(1)}, u32[]{:S(2)}, u32[]{:S(2)}) %collective-permute-start) | collective-permute-done | bytes 491552 | tf_op jit(solution)/shard_map/ppermute | solution.py:16
  28.0 0.5 collective-permute-start.2
  28.5 38.1 %collective-permute-done.1 = bf16[40,6144]{1,0:T(8,128)(2,1)S(1)} collective-permute-done((bf16[40,6144]{1,0:T(8,128)(2,1)}, bf16[40,6144]{1,0:T(8,128)(2,1)S(1)}, u32[]{:S(2)}, u32[]{:S(2)}) %collective-permute-start.1) | collective-permute-done | bytes 491552 | tf_op jit(solution)/shard_map/ppermute | solution.py:21
  66.7 1.6 collective-permute-done.2
  68.3 6.9 %fusion = f32[160,1024]{1,0:T(8,128)S(1)} fusion(bf16[160,6144]{1,0:T(8,128)(2,1)S(1)} %constant_dynamic-update-slice_fusion, bf16[1,6144,1024]{2,1,0:T(8,128)(2,1)} %param.11), kind=kOutput, calls=%fused_computation | convolution fusion | flops 2013265920 | bytes 15204352 | tf_op jit(solution)/shard_map/dot_general | solution.py:63
  75.3 0.1 slice-done.2
  75.4 2.2 fusion.2
  77.6 2.6 all-gather.2.cloned.1.call-done
  80.3 10.4 %fusion.7 = (f32[160]{0:T(256)S(1)}, bf16[160,1024]{1,0:T(8,128)(2,1)}, f32[160,1024]{1,0:T(8,128)}) fusion(f32[160,1024]{1,0:T(8,128)S(1)} %fusion.2, f32[160,1024]{1,0:T(8,128)S(1)} %fusion, bf16[160,6144]{1,0:T(8,128)(2,1)} %all-gather.2.cloned.1.call-done, bf16[1,1024,6144]{2,1,0:T(8,128)(2,1)} %param.13), kind=kOutput, calls=%fused_computation.16 | convolution fusion | flops 2014740352 | bytes 16843392 | tf_op jit(solution)/shard_map/dot_general | solution.py:68
  90.6 0.1 broadcast_in_dim.28
  90.7 41.7 %all-reduce.1 = f32[16,40]{1,0:T(8,128)S(1)} all-reduce(f32[16,40]{1,0:T(8,128)S(1)} %bitcast.66), channel_id=3, replica_groups=mesh['seq'=4,'exp'=2,'hid'=4] {'seq','hid'}, use_global_device_ids=true, to_apply=%region_7.8.clone | all-reduce | flops 640 | bytes 5120
  132.4 0.7 dynamic-slice_bitcast_fusion
  133.1 0.1 select_reduce_fusion
  133.2 0.2 dynamic-update-slice
  133.5 8.5 %all-reduce = bf16[160]{0:T(256)(128)(2,1)S(1)} all-reduce(bf16[160]{0:T(256)(128)(2,1)S(1)} %dynamic-update-slice), channel_id=1, replica_groups=mesh['seq'=4,'exp'=2,'hid'=4] {'seq'}, use_global_device_ids=true, to_apply=%add | all-reduce | flops 160 | bytes 640
  142.0 1.4 multiply_convert_fusion.1
  143.5 9.0 %fusion.15 = f32[4,40,4,1536]{3,1,2,0:T(8,128)S(1)} fusion(bf16[4,40,1024,1]{2,1,3,0:T(8,128)(2,1)S(1)} %bitcast.64, bf16[4,1536,1024,1]{2,1,0,3:T(8,128)(2,1)} %bitcast.59), kind=kOutput, calls=%fused_computation.40 | convolution fusion | flops 2013265920 | bytes 16842752 | tf_op jit(solution)/shard_map/sqf,hcf->shqc/dot_general | solution.py:89
  152.5 10.8 %convolution_add_fusion = f32[4,40,4,1536]{3,1,2,0:T(8,128)} fusion(f32[4,40,4,1536]{3,1,2,0:T(8,128)S(1)} %fusion.15, bf16[4,40,1024,1]{2,1,3,0:T(8,128)(2,1)S(1)} %bitcast.65, bf16[4,1536,1024,1]{2,1,0,3:T(8,128)(2,1)} %bitcast.60), kind=kOutput, calls=%fused_computation.11 | convolution fusion | flops 2014248960 | bytes 20774912 | tf_op jit(solution)/shard_map/sqf,hcf->shqc/dot_general | solution.py:95
  163.3 0.0 all-reduce.4.cloned.1.call-start
  163.4 2.7 psum.15
  166.1 0.6 convert_element_type.76
  166.6 6.6 %convert_bitcast_fusion.1 = bf16[1,6144,1024]{2,1,0:T(8,128)(2,1)} fusion(bf16[160,6144]{1,0:T(8,128)(2,1)S(1)} %constant_dynamic-update-slice_fusion, bf16[160,1024]{1,0:T(8,128)(2,1)S(1)} %copy-done.8), kind=kOutput, calls=%fused_computation.7 | convolution fusion | flops 2019557376 | bytes 14876672 | tf_op jit(solution)/shard_map/dot_general | solution.py:84
  173.3 6.6 %convert_bitcast_fusion.2 = bf16[1,6144,1024]{2,1,0:T(8,128)(2,1)} fusion(bf16[160,6144]{1,0:T(8,128)(2,1)S(1)} %constant_dynamic-update-slice_fusion, bf16[160,1024]{1,0:T(8,128)(2,1)S(1)} %copy-done.6), kind=kOutput, calls=%fused_computation.8 | convolution fusion | flops 2019557376 | bytes 14876672 | tf_op jit(solution)/shard_map/dot_general | solution.py:81
  179.9 116.2 %reduce-scatter.2.cloned.1.call-done = f32[1,40,1536]{2,1,0:T(8,128)} async-done(((f32[16,40,1536]{2,1,0:T(8,128)}), f32[1,40,1536]{2,1,0:T(8,128)}) %reduce-scatter.2.cloned.1.call-update) | async-done | bytes 245776 | tf_op jit(solution)/shard_map/reduce_scatter | solution.py:107
  296.1 2.5 convolution_convert_fusion.2
  298.7 10.1 %convert_bitcast_fusion = bf16[1,1024,6144]{2,1,0:T(8,128)(2,1)} fusion(bf16[160,6144]{1,0:T(8,128)(2,1)} %all-gather.2.cloned.1.call-done, bf16[160,1024]{1,0:T(8,128)(2,1)} %get-tuple-element.8, f32[160]{0:T(256)S(1)} %convert_element_type.63), kind=kOutput, calls=%fused_computation.6 | convolution fusion | flops 2020048896 | bytes 14877312 | tf_op jit(solution)/shard_map/dot_general | solution.py:73
  308.8 8.0 %all-reduce.4.cloned.1.call-done = bf16[128,1536]{1,0:T(8,128)(2,1)} async-done(((bf16[128,1536]{1,0:T(8,128)(2,1)}), bf16[128,1536]{1,0:T(8,128)(2,1)}) %all-reduce.4.cloned.1.call-update) | async-done | bytes 393232 | tf_op jit(solution)/shard_map/psum | solution.py:117
  316.7 2.0 convert_element_type.74
  (41 shorter events, 0.3 us)
Async XLA Ops:
  7.2 2.3 copy-start
  7.2 73.1 %all-gather.2.cloned.1.call-start = ((), (), s32[]{:S(2)}) async-start(), calls=%async_computation.1 | async-start | bytes 2457600 | tf_op jit(solution)/shard_map/all_gather | solution.py:55
  9.2 6.4 %copy-start.3 = (f32[128,40]{0,1:T(8,128)}, f32[128,40]{0,1:T(8,128)S(1)}, u32[]{:S(2)}) copy-start(f32[128,40]{0,1:T(8,128)S(1)} %convert_reduce_fusion) | copy-start | bytes 61444
  9.2 6.4 %copy-start.2 = (bf16[128,6144]{1,0:T(8,128)(2,1)S(1)}, bf16[128,6144]{1,0:T(8,128)(2,1)}, u32[]{:S(2)}) copy-start(bf16[128,6144]{1,0:T(8,128)(2,1)} %param.8) | copy-start | bytes 4718596
  10.6 6.3 %copy-start.11 = (u32[32]{0:T(128)S(1)}, u32[32]{0:T(128)}, u32[]{:S(2)}) copy-start(u32[32]{0:T(128)} %constant.68) | copy-start | bytes 388
  10.6 6.9 %copy-start.10 = (u32[32]{0:T(128)S(1)}, u32[32]{0:T(128)}, u32[]{:S(2)}) copy-start(u32[32]{0:T(128)} %constant.62) | copy-start | bytes 388
  10.6 17.4 %collective-permute-start = (bf16[40,6144]{1,0:T(8,128)(2,1)}, bf16[40,6144]{1,0:T(8,128)(2,1)S(1)}, u32[]{:S(2)}, u32[]{:S(2)}) collective-permute-start(bf16[40,6144]{1,0:T(8,128)(2,1)} %get-tuple-element.14), channel_id=1, source_target_pairs={{0,8},{8,16},{16,24},{24,0},{1,9},{9,17},{17,25},{25,1},{2,10},{10... | collective-permute-start | bytes 1474568 | tf_op jit(solution)/shard_map/ppermute | solution.py:16
  13.6 53.0 %collective-permute-start.1 = (bf16[40,6144]{1,0:T(8,128)(2,1)}, bf16[40,6144]{1,0:T(8,128)(2,1)S(1)}, u32[]{:S(2)}, u32[]{:S(2)}) collective-permute-start(bf16[40,6144]{1,0:T(8,128)(2,1)} %get-tuple-element.14), channel_id=1, source_target_pairs={{0,24},{8,0},{16,8},{24,16},{1,25},{9,1},{17,9},{25,17},{2,26},{10... | collective-permute-start | bytes 1474568 | tf_op jit(solution)/shard_map/ppermute | solution.py:21
  16.8 279.3 %reduce-scatter.2.cloned.1.call-start = ((), (), s32[]{:S(2)}) async-start(), calls=%async_computation.2 | async-start | bytes 4177920 | tf_op jit(solution)/shard_map/reduce_scatter | solution.py:107
  28.0 40.3 %collective-permute-start.2 = (bf16[40,6144]{1,0:T(8,128)(2,1)S(1)}, bf16[40,6144]{1,0:T(8,128)(2,1)S(1)}, u32[]{:S(2)}, u32[]{:S(2)}) collective-permute-start(bf16[40,6144]{1,0:T(8,128)(2,1)S(1)} %collective-permute-done), channel_id=1, source_target_pairs={{0,8},{8,16},{16,24},{24,0},{1,9},{9,17},{17,25},{25,1},{2,10},{10... | collective-permute-start | bytes 1474568 | tf_op jit(solution)/shard_map/ppermute | solution.py:16
  66.6 8.6 %slice-start = ((s8[12582912]{0:T(1024)(128)(4,1)}), s8[4194304]{0:T(1024)(128)(4,1)S(1)}, s32[]{:S(2)}) async-start(s8[12582912]{0:T(1024)(128)(4,1)} %bitcast.61), calls=%async_computation.4 | async-start | bytes 8388608
  68.3 7.0 %slice-start.1 = ((s8[12582912]{0:T(1024)(128)(4,1)}), s8[4194304]{0:T(1024)(128)(4,1)S(1)}, s32[]{:S(2)}) async-start(s8[12582912]{0:T(1024)(128)(4,1)} %bitcast.61), calls=%async_computation.5 | async-start | bytes 8388608
  68.3 7.1 %slice-start.2 = ((s8[12582912]{0:T(1024)(128)(4,1)}), s8[4194304]{0:T(1024)(128)(4,1)S(1)}, s32[]{:S(2)}) async-start(s8[12582912]{0:T(1024)(128)(4,1)} %bitcast.61), calls=%async_computation.6 | async-start | bytes 8388608
  77.6 55.5 %copy-start.9 = (f32[128,2]{0,1:T(2,128)S(1)}, f32[128,2]{0,1:T(2,128)}, u32[]{:S(2)}) copy-start(f32[128,2]{0,1:T(2,128)} %param.10) | copy-start | bytes 3076
  143.4 9.0 %copy-start.5 = (bf16[160,1024]{1,0:T(8,128)(2,1)}, bf16[160,1024]{1,0:T(8,128)(2,1)S(1)}, u32[]{:S(2)}) copy-start(bf16[160,1024]{1,0:T(8,128)(2,1)S(1)} %get-tuple-element.12) | copy-start | bytes 983044
  143.5 9.0 %copy-start.7 = (bf16[160,1024]{1,0:T(8,128)(2,1)}, bf16[160,1024]{1,0:T(8,128)(2,1)S(1)}, u32[]{:S(2)}) copy-start(bf16[160,1024]{1,0:T(8,128)(2,1)S(1)} %get-tuple-element.11) | copy-start | bytes 983044
  163.3 3.3 %copy-start.8 = (bf16[160,1024]{1,0:T(8,128)(2,1)S(1)}, bf16[160,1024]{1,0:T(8,128)(2,1)}, u32[]{:S(2)}) copy-start(bf16[160,1024]{1,0:T(8,128)(2,1)} %copy-done.7) | copy-start | bytes 983044
  163.3 153.4 %all-reduce.4.cloned.1.call-start = ((), (), s32[]{:S(2)}) async-start(), calls=%async_computation.3 | async-start | bytes 786432 | tf_op jit(solution)/shard_map/psum | solution.py:117
  166.6 6.6 %copy-start.6 = (bf16[160,1024]{1,0:T(8,128)(2,1)S(1)}, bf16[160,1024]{1,0:T(8,128)(2,1)}, u32[]{:S(2)}) copy-start(bf16[160,1024]{1,0:T(8,128)(2,1)} %copy-done.5) | copy-start | bytes 983044
  173.3 122.8 %copy-start.4 = (f32[128,40]{0,1:T(8,128)S(1)}, f32[128,40]{0,1:T(8,128)}, u32[]{:S(2)}) copy-start(f32[128,40]{0,1:T(8,128)} %copy-done.3) | copy-start | bytes 61444
  298.7 20.0 %copy-start.1 = (bf16[128,6144]{1,0:T(8,128)(2,1)S(1)}, bf16[128,6144]{1,0:T(8,128)(2,1)}, u32[]{:S(2)}) copy-start(bf16[128,6144]{1,0:T(8,128)(2,1)} %param.7) | copy-start | bytes 4718596
Sparse Core Ops, SparseCore 0:
  16.9 63.2 all-gather.1
  163.5 132.6 reduce-scatter.1
  299.0 17.6 all-reduce.3
